TPU v7x, 32 devices: a whole 2x2x4 slice. The times are simulated.
32 devices in a mesh: fsdp: 2 (over x), ctx: 4 (over y, core), tp: 4 (over z).
Axes of the slice: x: 2, y: 2, z: 4, core: 2. Of those that a mesh axis runs over, the one named last changes fastest.
Arguments:
- tokens: bfloat16 [2048, 4, 1024], P(('ctx', 'tp'), 'fsdp'), may hold values from -6 to 6
- segment_ids: int32 [4, 2048], P('fsdp', 'ctx'), may hold values from 0 to 5, never falling along the last dimension, each value on 1 to 800 neighbouring positions
- decay_rate: float32 [8], P('tp'), may hold values from 0.0005 to 0.07
- w_query: float32 [1024, 1024], P(('fsdp', 'ctx'), 'tp'), may hold values from -0.1875 to 0.1875
- w_key: float32 [1024, 1024], P(('fsdp', 'ctx'), 'tp'), may hold values from -0.1875 to 0.1875
- w_value: float32 [1024, 1024], P(('fsdp', 'ctx'), 'tp'), may hold values from -0.1875 to 0.1875
- w_gate: float32 [1024, 1024], P(('fsdp', 'ctx'), 'tp'), may hold values from -0.1875 to 0.1875
- w_out: float32 [1024, 1024], P('tp', ('fsdp', 'ctx')), may hold values from -0.375 to 0.375
- glu_left: float32 [1024, 2816], P(('fsdp', 'ctx'), 'tp'), may hold values from -0.1875 to 0.1875
- glu_right: float32 [1024, 2816], P(('fsdp', 'ctx'), 'tp'), may hold values from -0.1875 to 0.1875
- glu_down: float32 [2816, 1024], P('tp', ('fsdp', 'ctx')), may hold values from -0.109375 to 0.109375
- cotangent: bfloat16 [2048, 4, 1024], P(('ctx', 'tp'), 'fsdp'), may hold values from -6 to 6
Outputs:
- output: bfloat16 [2048, 4, 1024], P(('ctx', 'tp'), 'fsdp')
- grad_tokens: float32 [2048, 4, 1024], P(('ctx', 'tp'), 'fsdp')
- grad_query: float32 [1024, 1024], P(('fsdp', 'ctx'), 'tp')
- grad_key: float32 [1024, 1024], P(('fsdp', 'ctx'), 'tp')
- grad_value: float32 [1024, 1024], P(('fsdp', 'ctx'), 'tp')
- grad_gate: float32 [1024, 1024], P(('fsdp', 'ctx'), 'tp')
- grad_out: float32 [1024, 1024], P('tp', ('fsdp', 'ctx'))
- grad_left: float32 [1024, 2816], P(('fsdp', 'ctx'), 'tp')
- grad_right: float32 [1024, 2816], P(('fsdp', 'ctx'), 'tp')
- grad_down: float32 [2816, 1024], P('tp', ('fsdp', 'ctx'))
Inputs may be any that keep to these rules, and one draw needn't show every extreme that they name: `segment_ids`: along each sequence the document numbers never fall; every document has 1 to 800 tokens and one has exactly 800.
All inputs are finite; a program needn't handle non-finite values.
Results may differ from a plain program's by a relative error of at most 0.013.
Values may be sent and summed in bfloat16 or wider, within the bound.
A program may use at most 128 MiB of HBM per device.

v0:
```python
import jax
import jax.numpy as jnp
from jax import lax
from jax.sharding import PartitionSpec as P

DH = 128
EPSILON = 1e-06
HEAD_FLOOR = 1.0
HIGHEST = lax.Precision.HIGHEST


def entering(x, axis, join, neutral):
    place = lax.axis_index(axis)
    gathered = jax.tree.map(
        lambda a, kind: lax.all_gather(a.astype(kind), axis),
        x,
        (jnp.bfloat16, jnp.bfloat16, jnp.bfloat16, jnp.bfloat16),
    )
    state = jax.tree.map(lambda a, e: jnp.zeros_like(a) + jnp.asarray(e, a.dtype), x, neutral)

    def one(lap, state):
        return join(
            state,
            jax.tree.map(
                lambda a, own: lax.dynamic_index_in_dim(a, lap, 0, False).astype(own.dtype),
                gathered,
                x,
            ),
        )

    return lax.fori_loop(0, place, one, state)


def entering_2(x, axis, join, neutral):
    count = lax.axis_size(axis)
    place = lax.axis_index(axis)
    ahead = count - 1 - place
    gathered = jax.tree.map(
        lambda a, kind: lax.all_gather(a.astype(kind), axis), x, (jnp.bfloat16, jnp.bfloat16)
    )
    state = jax.tree.map(lambda a, e: jnp.zeros_like(a) + jnp.asarray(e, a.dtype), x, neutral)

    def one(lap, state):
        source = count - 1 - lap
        return join(
            state,
            jax.tree.map(
                lambda a, own: lax.dynamic_index_in_dim(a, source, 0, False).astype(own.dtype),
                gathered,
                x,
            ),
        )

    return lax.fori_loop(0, ahead, one, state)


def normalize(values, floor_value=EPSILON):
    return values * lax.rsqrt(jnp.mean(values * values, axis=-1, keepdims=True) + floor_value)


def norm_backward(values, upstream, floor_value=EPSILON):
    inverse = lax.rsqrt(jnp.mean(values * values, axis=-1, keepdims=True) + floor_value)
    inner_mean = jnp.mean(upstream * values, axis=-1, keepdims=True)
    return inverse * (upstream - values * inner_mean * inverse * inverse)


def silu_slope(values):
    sigmoid_value = jax.nn.sigmoid(values)
    return sigmoid_value * (1.0 + values * (1.0 - sigmoid_value))


def chain_forward(earlier, later):
    early_first, early_last, early_decay, early_state = earlier
    late_first, late_last, late_decay, late_state = later
    linked = (late_first == early_last) | (early_last < 0.0) | (late_first < 0.0)
    carried = jnp.where(linked[:, None], late_decay, 0.0)
    first_seg = jnp.where(early_first < 0.0, late_first, early_first)
    last_seg = jnp.where(late_last < 0.0, early_last, late_last)
    return (
        first_seg,
        last_seg,
        early_decay * carried,
        late_state + carried[:, :, None, None] * early_state,
    )


def chain_backward(earlier, later):
    return (earlier[0] * later[0], later[1] + later[0][:, :, None, None] * earlier[1])


def shards(
    tokens,
    segment_ids,
    decay_rate,
    w_query,
    w_key,
    w_value,
    w_gate,
    w_out,
    glu_left,
    glu_right,
    glu_down,
    cotangent,
):
    shard_len, seq_count, model_width = tokens.shape
    tok_float = tokens.astype(jnp.float32)
    normed_part = normalize(tok_float).astype(jnp.bfloat16)
    gathered = (
        lax.all_gather(w_query.astype(jnp.bfloat16), ("fsdp", "ctx"), axis=0, tiled=True),
        lax.all_gather(w_key.astype(jnp.bfloat16), ("fsdp", "ctx"), axis=0, tiled=True),
        lax.all_gather(w_value.astype(jnp.bfloat16), ("fsdp", "ctx"), axis=0, tiled=True),
        lax.all_gather(w_gate.astype(jnp.bfloat16), ("fsdp", "ctx"), axis=0, tiled=True),
        lax.all_gather(w_out.astype(jnp.bfloat16), ("fsdp", "ctx"), axis=1, tiled=True),
        lax.all_gather(glu_left.astype(jnp.bfloat16), ("fsdp", "ctx"), axis=0, tiled=True),
        lax.all_gather(glu_right.astype(jnp.bfloat16), ("fsdp", "ctx"), axis=0, tiled=True),
        lax.all_gather(glu_down.astype(jnp.bfloat16), ("fsdp", "ctx"), axis=1, tiled=True),
    )
    full_query, full_key, full_value, full_gate, full_out, full_left, full_right, full_down = (
        gathered
    )
    normed = lax.all_gather(normed_part, "tp", axis=0, tiled=True)
    block_len = normed.shape[0]
    total_rows = block_len * seq_count
    normed_flat = normed.reshape(total_rows, model_width)
    local_width = full_query.shape[1]
    head_count = local_width // DH
    head_shape = (block_len, seq_count, head_count, DH)
    proj_query = jnp.dot(normed_flat, full_query, preferred_element_type=jnp.float32)
    proj_key = jnp.dot(normed_flat, full_key, preferred_element_type=jnp.float32)
    proj_value = jnp.dot(normed_flat, full_value, preferred_element_type=jnp.float32)
    proj_gate = jnp.dot(normed_flat, full_gate, preferred_element_type=jnp.float32)
    queries = jax.nn.silu(proj_query).astype(jnp.bfloat16).reshape(head_shape)
    keys_low = jax.nn.silu(proj_key).astype(jnp.bfloat16).reshape(head_shape)
    values_low = proj_value.astype(jnp.bfloat16).reshape(head_shape)
    seg_pos = segment_ids.T
    seg_float = seg_pos.astype(jnp.float32)
    position = jnp.arange(block_len).astype(jnp.float32)
    distance = position[:, None] - position[None, :]
    same_doc = (segment_ids[:, :, None] == segment_ids[:, None, :]) & (distance >= 0.0)[None]
    decay_grid = jnp.where(
        same_doc[:, None],
        jnp.exp(-decay_rate[None, :, None, None] * jnp.maximum(distance, 0.0)[None, None]),
        0.0,
    )
    end_weight = jnp.where(
        (seg_pos == seg_pos[-1:])[:, :, None],
        jnp.exp(-(block_len - 1.0 - position)[:, None, None] * decay_rate[None, None, :]),
        0.0,
    )
    keys_end = (keys_low.astype(jnp.float32) * end_weight[..., None]).astype(jnp.bfloat16)
    update = jnp.einsum("tbhd,tbhe->bhde", keys_end, values_low, preferred_element_type=jnp.float32)
    first_seg = seg_float[0]
    last_seg = seg_float[-1]
    span_decay = jnp.where(
        (first_seg == last_seg)[:, None], jnp.exp(-block_len * decay_rate)[None, :], 0.0
    )
    identity = (
        -jnp.ones((seq_count,), jnp.float32),
        -jnp.ones((seq_count,), jnp.float32),
        jnp.ones((seq_count, head_count), jnp.float32),
        jnp.zeros((seq_count, head_count, DH, DH), jnp.float32),
    )
    scanned = entering((first_seg, last_seg, span_decay, update), "ctx", chain_forward, identity)
    prior_last = scanned[1]
    state_low = scanned[3].astype(jnp.bfloat16)
    inflow = jnp.where(
        (seg_pos == prior_last[None, :])[:, :, None],
        jnp.exp(-(position + 1.0)[:, None, None] * decay_rate[None, None, :]),
        0.0,
    )
    scores = jnp.einsum("tbhd,sbhd->bhts", queries, keys_low, preferred_element_type=jnp.float32)
    weights_low = (scores * decay_grid).astype(jnp.bfloat16)
    intra = jnp.einsum(
        "bhts,sbhd->tbhd", weights_low, values_low, preferred_element_type=jnp.float32
    )
    inter = (
        jnp.einsum("tbhd,bhde->tbhe", queries, state_low, preferred_element_type=jnp.float32)
        * inflow[..., None]
    )
    attended = intra + inter
    attended_norm = normalize(attended, HEAD_FLOOR)
    gate_value = jax.nn.sigmoid(proj_gate).reshape(head_shape)
    mixed_heads = (
        (attended_norm * gate_value).astype(jnp.bfloat16).reshape(block_len, seq_count, local_width)
    )
    row_count = shard_len * lax.axis_size("tp")
    piece_rows = mixed_heads.reshape(row_count * seq_count, local_width)
    branch = lax.psum_scatter(
        jnp.dot(piece_rows, full_out, preferred_element_type=jnp.float32).reshape(
            row_count, seq_count, model_width
        ),
        "tp",
        scatter_dimension=0,
        tiled=True,
    )
    residual = tok_float + branch
    second_part = normalize(residual).astype(jnp.bfloat16)
    second = lax.all_gather(second_part, "tp", axis=0, tiled=True)
    second_flat = second.reshape(total_rows, model_width)
    left_proj = jnp.dot(second_flat, full_left, preferred_element_type=jnp.float32)
    right_proj = jnp.dot(second_flat, full_right, preferred_element_type=jnp.float32)
    hidden = (left_proj * right_proj).astype(jnp.bfloat16)
    ffn_width = hidden.shape[1]
    hidden_blocks = hidden.reshape(block_len, seq_count, ffn_width)
    row_count = shard_len * lax.axis_size("tp")
    piece_rows = hidden_blocks.reshape(row_count * seq_count, ffn_width)
    ffn_branch = lax.psum_scatter(
        jnp.dot(piece_rows, full_down, preferred_element_type=jnp.float32)
        .reshape(row_count, seq_count, model_width)
        .astype(jnp.bfloat16),
        "tp",
        scatter_dimension=0,
        tiled=True,
    ).astype(jnp.float32)
    output = (residual + ffn_branch).astype(jnp.bfloat16)
    upstream = lax.all_gather(cotangent, "tp", axis=0, tiled=True).reshape(total_rows, model_width)
    grad_down = jnp.dot(hidden.T, upstream, preferred_element_type=jnp.float32)
    grad_hidden = jnp.dot(upstream, full_down.T, preferred_element_type=jnp.float32)
    grad_left_proj = (grad_hidden * right_proj).astype(jnp.bfloat16)
    grad_right_proj = (grad_hidden * left_proj).astype(jnp.bfloat16)
    grad_left = jnp.dot(second_flat.T, grad_left_proj, preferred_element_type=jnp.float32)
    grad_right = jnp.dot(second_flat.T, grad_right_proj, preferred_element_type=jnp.float32)
    left_blocks = grad_left_proj.reshape(block_len, seq_count, ffn_width)
    right_blocks = grad_right_proj.reshape(block_len, seq_count, ffn_width)
    row_count = shard_len * lax.axis_size("tp")
    left_rows = left_blocks.reshape(row_count * seq_count, ffn_width)
    right_rows = right_blocks.reshape(row_count * seq_count, ffn_width)
    summed = jnp.dot(left_rows, full_left.T, preferred_element_type=jnp.float32) + jnp.dot(
        right_rows, full_right.T, preferred_element_type=jnp.float32
    )
    grad_second = lax.psum_scatter(
        summed.reshape(row_count, seq_count, model_width), "tp", scatter_dimension=0, tiled=True
    )
    grad_residual = cotangent.astype(jnp.float32) + norm_backward(residual, grad_second)
    branch_low = grad_residual.astype(jnp.bfloat16)
    grad_branch = lax.all_gather(branch_low, "tp", axis=0, tiled=True).reshape(
        total_rows, model_width
    )
    grad_wout = jnp.dot(
        mixed_heads.reshape(total_rows, local_width).T,
        grad_branch,
        preferred_element_type=jnp.float32,
    )
    grad_mixed = jnp.dot(grad_branch, full_out.T, preferred_element_type=jnp.float32).reshape(
        head_shape
    )
    grad_gate_proj = (
        (grad_mixed * attended_norm * gate_value * (1.0 - gate_value))
        .astype(jnp.bfloat16)
        .reshape(total_rows, local_width)
    )
    grad_attended = norm_backward(attended, grad_mixed * gate_value, HEAD_FLOOR).astype(
        jnp.bfloat16
    )
    grad_weights = jnp.einsum(
        "tbhd,sbhd->bhts", grad_attended, values_low, preferred_element_type=jnp.float32
    )
    grad_scores = (grad_weights * decay_grid).astype(jnp.bfloat16)
    grad_queries = jnp.einsum(
        "bhts,sbhd->tbhd", grad_scores, keys_low, preferred_element_type=jnp.float32
    )
    grad_queries = (
        grad_queries
        + jnp.einsum(
            "tbhe,bhde->tbhd", grad_attended, state_low, preferred_element_type=jnp.float32
        )
        * inflow[..., None]
    )
    grad_keys = jnp.einsum(
        "bhts,tbhd->sbhd", grad_scores, queries, preferred_element_type=jnp.float32
    )
    grad_values = jnp.einsum(
        "bhts,tbhd->sbhd", weights_low, grad_attended, preferred_element_type=jnp.float32
    )
    weighted_queries = queries.astype(jnp.float32) * inflow[..., None]
    grad_prior_local = jnp.einsum(
        "tbhd,tbhe->bhde", weighted_queries, grad_attended.astype(jnp.float32), precision=HIGHEST
    )
    link_decay = jnp.where((first_seg == prior_last)[:, None], span_decay, 0.0)
    back_identity = (
        jnp.ones((seq_count, head_count), jnp.float32),
        jnp.zeros((seq_count, head_count, DH, DH), jnp.float32),
    )
    grad_update = entering_2((link_decay, grad_prior_local), "ctx", chain_backward, back_identity)[
        1
    ]
    grad_values = grad_values + jnp.einsum(
        "tbhd,bhde->tbhe", keys_end.astype(jnp.float32), grad_update, precision=HIGHEST
    )
    grad_keys = (
        grad_keys
        + jnp.einsum(
            "tbhe,bhde->tbhd", values_low.astype(jnp.float32), grad_update, precision=HIGHEST
        )
        * end_weight[..., None]
    )
    grad_query_proj = (
        (grad_queries * silu_slope(proj_query).reshape(head_shape))
        .astype(jnp.bfloat16)
        .reshape(total_rows, local_width)
    )
    grad_key_proj = (
        (grad_keys * silu_slope(proj_key).reshape(head_shape))
        .astype(jnp.bfloat16)
        .reshape(total_rows, local_width)
    )
    grad_value_proj = grad_values.astype(jnp.bfloat16).reshape(total_rows, local_width)
    grad_wquery = jnp.dot(normed_flat.T, grad_query_proj, preferred_element_type=jnp.float32)
    grad_wkey = jnp.dot(normed_flat.T, grad_key_proj, preferred_element_type=jnp.float32)
    grad_wvalue = jnp.dot(normed_flat.T, grad_value_proj, preferred_element_type=jnp.float32)
    grad_wgate = jnp.dot(normed_flat.T, grad_gate_proj, preferred_element_type=jnp.float32)
    query_blocks = grad_query_proj.reshape(block_len, seq_count, local_width)
    key_blocks = grad_key_proj.reshape(block_len, seq_count, local_width)
    value_blocks = grad_value_proj.reshape(block_len, seq_count, local_width)
    gate_blocks = grad_gate_proj.reshape(block_len, seq_count, local_width)
    row_count = shard_len * lax.axis_size("tp")
    summed = jnp.zeros((row_count * seq_count, model_width), jnp.float32)
    for grad_blocks, weight_full in (
        (query_blocks, full_query),
        (key_blocks, full_key),
        (value_blocks, full_value),
        (gate_blocks, full_gate),
    ):
        piece_rows = grad_blocks.reshape(row_count * seq_count, local_width)
        summed = summed + jnp.dot(piece_rows, weight_full.T, preferred_element_type=jnp.float32)
    grad_normed = lax.psum_scatter(
        summed.reshape(row_count, seq_count, model_width).astype(jnp.bfloat16),
        "tp",
        scatter_dimension=0,
        tiled=True,
    ).astype(jnp.float32)
    grad_tokens = grad_residual + norm_backward(tok_float, grad_normed)
    every_grad = (
        lax.psum_scatter(grad_wquery, ("fsdp", "ctx"), scatter_dimension=0, tiled=True),
        lax.psum_scatter(grad_wkey, ("fsdp", "ctx"), scatter_dimension=0, tiled=True),
        lax.psum_scatter(grad_wvalue, ("fsdp", "ctx"), scatter_dimension=0, tiled=True),
        lax.psum_scatter(grad_wgate, ("fsdp", "ctx"), scatter_dimension=0, tiled=True),
        lax.psum_scatter(grad_wout, ("fsdp", "ctx"), scatter_dimension=1, tiled=True),
        lax.psum_scatter(grad_left, ("fsdp", "ctx"), scatter_dimension=0, tiled=True),
        lax.psum_scatter(grad_right, ("fsdp", "ctx"), scatter_dimension=0, tiled=True),
        lax.psum_scatter(grad_down, ("fsdp", "ctx"), scatter_dimension=1, tiled=True),
    )
    return (
        output,
        grad_tokens,
        every_grad[0],
        every_grad[1],
        every_grad[2],
        every_grad[3],
        every_grad[4],
        every_grad[5],
        every_grad[6],
        every_grad[7],
    )


def solution(mesh):
    in_specs = (
        P(("ctx", "tp"), "fsdp", None),
        P("fsdp", "ctx"),
        P("tp"),
        P(("fsdp", "ctx"), "tp"),
        P(("fsdp", "ctx"), "tp"),
        P(("fsdp", "ctx"), "tp"),
        P(("fsdp", "ctx"), "tp"),
        P("tp", ("fsdp", "ctx")),
        P(("fsdp", "ctx"), "tp"),
        P(("fsdp", "ctx"), "tp"),
        P("tp", ("fsdp", "ctx")),
        P(("ctx", "tp"), "fsdp", None),
    )
    out_specs = (
        P(("ctx", "tp"), "fsdp", None),
        P(("ctx", "tp"), "fsdp", None),
        P(("fsdp", "ctx"), "tp"),
        P(("fsdp", "ctx"), "tp"),
        P(("fsdp", "ctx"), "tp"),
        P(("fsdp", "ctx"), "tp"),
        P("tp", ("fsdp", "ctx")),
        P(("fsdp", "ctx"), "tp"),
        P(("fsdp", "ctx"), "tp"),
        P("tp", ("fsdp", "ctx")),
    )
    return jax.shard_map(shards, mesh=mesh, in_specs=in_specs, out_specs=out_specs, check_vma=False)
```

profile of v0, /device:TPU:0, one launch (start us, length us, event | category | flops | bytes accessed | tf_op | source)
XLA Modules:
  0.0 1034.6 jit_solution(431356184398698397)
XLA Ops:
  11.0 6.0 all-gather.3
  17.2 5.3 all-gather.2
  22.5 5.0 all_gather.72
  28.1 10.1 all_gather.67
  38.2 9.8 all_gather.65
  48.0 9.9 all_gather.66
  57.9 10.7 %all_gather.73 = bf16[1024,256]{1,0:T(8,128)(2,1)} all-gather(bf16[128,256]{1,0:T(8,128)(2,1)S(1)} %convert_element_type.256), channel_id=1, replica_groups=mesh['fsdp'=2,'ctx'=4,'tp'=4] {'fsdp','ctx'}, dimensions={0}, use_global_device_ids=true | all-gather | bytes 589824 | tf_op jit(solution)/shard_map/all_gather | solution.py:112
  68.7 10.1 all_gather.74
  81.0 5.1 copy.98
  86.1 4.1 reshape.419
  90.3 3.7 add_multiply_fusion
  97.2 3.3 convolution_convert_fusion.1
  102.0 7.8 all-gather
  110.2 3.6 add_multiply_fusion.1
  123.0 2.7 reshape.423
  130.7 2.8 fusion.47
  134.3 80.6 %reduce-scatter.13.cloned.1.call-done = f32[128,2,1024]{2,0,1:T(8,128)} async-done(((f32[512,2,1024]{2,0,1:T(8,128)}), f32[128,2,1024]{2,0,1:T(8,128)}) %reduce-scatter.13.cloned.1.call-update) | async-done | bytes 1048592 | tf_op jit(solution)/shard_map/reduce_scatter | solution.py:188
  221.8 41.2 %all-gather.22.cloned.1.call-done = bf16[512,2,1024]{2,1,0:T(2,128)(2,1)} async-done(((bf16[128,2,1024]{2,1,0:T(2,128)(2,1)}), bf16[512,2,1024]{2,1,0:T(2,128)(2,1)}) %all-gather.22.cloned.1.call-update) | async-done | bytes 2097168 | tf_op jit(solution)/shard_map/all_gather | solution.py:216
  263.0 4.1 reshape.425
  267.1 42.1 %all-gather.14.cloned.1.call-done = bf16[512,2,1024]{2,0,1:T(8,128)(2,1)} async-done(((bf16[128,2,1024]{2,0,1:T(8,128)(2,1)}), bf16[512,2,1024]{2,0,1:T(8,128)(2,1)}) %all-gather.14.cloned.1.call-update) | async-done | bytes 2097168 | tf_op jit(solution)/shard_map/all_gather | solution.py:198
  309.2 5.2 copy.112
  314.4 4.1 reshape.424
  318.5 17.2 %all-gather.16.cloned.1.call-done = bf16[1024,704]{0,1:T(8,128)(2,1)} async-done(((bf16[128,704]{0,1:T(8,128)(2,1)}), bf16[1024,704]{0,1:T(8,128)(2,1)}) %all-gather.16.cloned.1.call-update) | async-done | bytes 1441808 | tf_op jit(solution)/shard_map/all_gather | solution.py:114
  335.7 5.3 fusion.68
  341.0 22.5 %all-gather.18.cloned.1.call-done = bf16[1024,704]{0,1:T(8,128)(2,1)} async-done(((bf16[128,704]{0,1:T(8,128)(2,1)}), bf16[1024,704]{0,1:T(8,128)(2,1)}) %all-gather.18.cloned.1.call-update) | async-done | bytes 1441808 | tf_op jit(solution)/shard_map/all_gather | solution.py:115
  363.5 5.2 fusion.69
  368.7 22.7 %all-gather.20.cloned.1.call-done = bf16[704,1024]{1,0:T(8,128)(2,1)} async-done(((bf16[704,128]{1,0:T(8,128)(2,1)}), bf16[704,1024]{1,0:T(8,128)(2,1)}) %all-gather.20.cloned.1.call-update) | async-done | bytes 1441808 | tf_op jit(solution)/shard_map/all_gather | solution.py:116
  391.4 6.8 multiply_convert_fusion
  400.6 3.9 convolution_add_fusion
  404.5 6.0 reshape.426
  410.5 5.5 copy.115
  416.1 76.9 %reduce-scatter.17.cloned.1.call-done = f32[128,2,1024]{2,0,1:T(8,128)} async-done(((f32[512,2,1024]{2,0,1:T(8,128)}), f32[128,2,1024]{2,0,1:T(8,128)}) %reduce-scatter.17.cloned.1.call-update) | async-done | bytes 1048592 | tf_op jit(solution)/shard_map/reduce_scatter | solution.py:231
  496.5 5.0 all_gather.83
  501.5 2.7 reshape.428
  506.6 2.8 reshape.427
  511.6 31.4 %all-gather.24.cloned.1.call-done = bf16[512,2,1024]{2,0,1:T(8,128)(2,1)} async-done(((bf16[128,2,1024]{2,0,1:T(8,128)(2,1)}), bf16[512,2,1024]{2,0,1:T(8,128)(2,1)}) %all-gather.24.cloned.1.call-update) | async-done | bytes 2097168 | tf_op jit(solution)/shard_map/all_gather | solution.py:236
  543.0 4.0 multiply_reduce_fusion
  554.6 7.3 all-gather.1
  565.9 4.1 fusion.41
  573.3 3.8 fusion.45
  578.2 2.8 fusion.37
  582.1 5.6 add_convert_fusion
  590.0 3.7 copy.135
  595.0 3.1 convolution_convert_fusion
  598.2 2.8 convert_element_type.265
  604.2 4.8 fusion.73
  610.4 4.9 fusion.74
  617.0 4.7 fusion.72
  624.0 3.5 copy.137
  627.5 2.7 reshape.429
  630.3 2.8 fusion.29
  633.2 3.4 fusion.39
  636.7 3.4 fusion.43
  640.1 3.3 fusion.35
  643.6 3.4 fusion.32
  648.5 33.1 %reduce-scatter.15.cloned.1.call-done = bf16[128,2,1024]{2,0,1:T(8,128)(2,1)} async-done(((bf16[512,2,1024]{2,0,1:T(8,128)(2,1)}), bf16[128,2,1024]{2,0,1:T(8,128)(2,1)}) %reduce-scatter.15.cloned.1.call-update) | async-done | bytes 524304 | tf_op jit(solution)/shard_map/reduce_scatter | solution.py:207
  686.6 43.0 %reduce-scatter.31.cloned.1.call-done = f32[128,704]{0,1:T(8,128)} async-done(((f32[1024,704]{0,1:T(8,128)}), f32[128,704]{0,1:T(8,128)}) %reduce-scatter.31.cloned.1.call-update) | async-done | bytes 360464 | tf_op jit(solution)/shard_map/reduce_scatter | solution.py:339
  729.6 49.2 %reduce-scatter.33.cloned.1.call-done = f32[128,704]{0,1:T(8,128)} async-done(((f32[1024,704]{0,1:T(8,128)}), f32[128,704]{0,1:T(8,128)}) %reduce-scatter.33.cloned.1.call-update) | async-done | bytes 360464 | tf_op jit(solution)/shard_map/reduce_scatter | solution.py:340
  778.9 48.7 %reduce-scatter.35.cloned.1.call-done = f32[704,128]{1,0:T(8,128)} async-done(((f32[704,1024]{1,0:T(8,128)}), f32[704,128]{1,0:T(8,128)}) %reduce-scatter.35.cloned.1.call-update) | async-done | bytes 360464 | tf_op jit(solution)/shard_map/reduce_scatter | solution.py:341
  827.6 40.0 %reduce-scatter.29.cloned.1.call-done = f32[256,128]{1,0:T(8,128)} async-done(((f32[256,1024]{1,0:T(8,128)}), f32[256,128]{1,0:T(8,128)}) %reduce-scatter.29.cloned.1.call-update) | async-done | bytes 131088 | tf_op jit(solution)/shard_map/reduce_scatter | solution.py:338
  867.6 40.0 %reduce-scatter.23.cloned.1.call-done = f32[128,256]{1,0:T(8,128)} async-done(((f32[1024,256]{1,0:T(8,128)}), f32[128,256]{1,0:T(8,128)}) %reduce-scatter.23.cloned.1.call-update) | async-done | bytes 131088 | tf_op jit(solution)/shard_map/reduce_scatter | solution.py:335
  907.6 40.0 %reduce-scatter.21.cloned.1.call-done = f32[128,256]{1,0:T(8,128)} async-done(((f32[1024,256]{1,0:T(8,128)}), f32[128,256]{1,0:T(8,128)}) %reduce-scatter.21.cloned.1.call-update) | async-done | bytes 131088 | tf_op jit(solution)/shard_map/reduce_scatter | solution.py:334
  947.6 40.0 %reduce-scatter.25.cloned.1.call-done = f32[128,256]{1,0:T(8,128)} async-done(((f32[1024,256]{1,0:T(8,128)}), f32[128,256]{1,0:T(8,128)}) %reduce-scatter.25.cloned.1.call-update) | async-done | bytes 131088 | tf_op jit(solution)/shard_map/reduce_scatter | solution.py:336
  987.5 40.1 %reduce-scatter.27.cloned.1.call-done = f32[128,256]{1,0:T(8,128)} async-done(((f32[1024,256]{1,0:T(8,128)}), f32[128,256]{1,0:T(8,128)}) %reduce-scatter.27.cloned.1.call-update) | async-done | bytes 131088 | tf_op jit(solution)/shard_map/reduce_scatter | solution.py:337
  (245 shorter events, 80.4 us)
Async XLA Ops:
  7.2 3.6 copy-start.54
  7.2 10.0 copy-start.55
  7.2 20.4 %copy-start.49 = (f32[128,256]{1,0:T(8,128)S(1)}, f32[128,256]{1,0:T(8,128)}, u32[]{:S(2)}) copy-start(f32[128,256]{1,0:T(8,128)} %param.20) | copy-start | bytes 393220
  7.2 20.4 %copy-start.50 = (f32[128,256]{1,0:T(8,128)S(1)}, f32[128,256]{1,0:T(8,128)}, u32[]{:S(2)}) copy-start(f32[128,256]{1,0:T(8,128)} %param.21) | copy-start | bytes 393220
  7.2 20.6 %copy-start.51 = (f32[128,256]{1,0:T(8,128)S(1)}, f32[128,256]{1,0:T(8,128)}, u32[]{:S(2)}) copy-start(f32[128,256]{1,0:T(8,128)} %param.19) | copy-start | bytes 393220
  7.2 20.6 %copy-start.52 = (f32[128,256]{1,0:T(8,128)S(1)}, f32[128,256]{1,0:T(8,128)}, u32[]{:S(2)}) copy-start(f32[128,256]{1,0:T(8,128)} %param.22) | copy-start | bytes 393220
  7.2 20.6 %copy-start.53 = (f32[256,128]{1,0:T(8,128)S(1)}, f32[256,128]{1,0:T(8,128)}, u32[]{:S(2)}) copy-start(f32[256,128]{1,0:T(8,128)} %param.23) | copy-start | bytes 393220
  7.2 73.8 %all-gather.12.cloned.1.call-start = ((), (), s32[]{:S(2)}) async-start(), calls=%async_computation.12 | async-start | bytes 2621440 | tf_op jit(solution)/shard_map/all_gather | solution.py:121
  10.7 204.1 %reduce-scatter.13.cloned.1.call-start = ((), (), s32[]{:S(2)}) async-start(), calls=%async_computation.13 | async-start | bytes 5242880 | tf_op jit(solution)/shard_map/reduce_scatter | solution.py:188
  38.2 52.1 %copy-start.38 = (bf16[1024,256]{1,0:T(8,128)(2,1)}, bf16[1024,256]{1,0:T(8,128)(2,1)S(1)}, u32[]{:S(2)}) copy-start(bf16[1024,256]{1,0:T(8,128)(2,1)S(1)} %all_gather.67) | copy-start | bytes 1572868
  48.0 49.2 %copy-start.36 = (bf16[1024,256]{1,0:T(8,128)(2,1)}, bf16[1024,256]{1,0:T(8,128)(2,1)S(1)}, u32[]{:S(2)}) copy-start(bf16[1024,256]{1,0:T(8,128)(2,1)S(1)} %all_gather.65) | copy-start | bytes 1572868
  97.2 18.8 %copy-start.13 = (bf16[512,2,2,128]{0,3,2,1:T(8,128)(2,1)}, bf16[512,2,2,128]{0,3,2,1:T(8,128)(2,1)S(1)}, u32[]{:S(2)}) copy-start(bf16[512,2,2,128]{0,3,2,1:T(8,128)(2,1)S(1)} %copy.103) | copy-start | bytes 1572868
  101.7 8.1 copy-start.15
  116.1 3.2 copy-start.8
  116.1 2.3 copy-start.16
  118.3 2.3 copy-start.4
  119.2 2.1 copy-start.46
  125.8 4.9 copy-start.23
  133.5 81.4 %copy-start = (bf16[128,2,1024]{2,1,0:T(2,128)(2,1)S(1)}, bf16[128,2,1024]{2,1,0:T(2,128)(2,1)}, u32[]{:S(2)}) copy-start(bf16[128,2,1024]{2,1,0:T(2,128)(2,1)} %param.16) | copy-start | bytes 1572868
  133.5 129.5 %all-gather.22.cloned.1.call-start = ((), (), s32[]{:S(2)}) async-start(), calls=%async_computation.19 | async-start | bytes 2621440 | tf_op jit(solution)/shard_map/all_gather | solution.py:216
  134.2 83.3 %copy-start.48 = (f32[128,704]{0,1:T(8,128)S(1)}, f32[128,704]{0,1:T(8,128)}, u32[]{:S(2)}) copy-start(f32[128,704]{0,1:T(8,128)} %param.24) | copy-start | bytes 1081348
  134.2 175.0 %all-gather.14.cloned.1.call-start = ((), (), s32[]{:S(2)}) async-start(), calls=%async_computation.14 | async-start | bytes 2621440 | tf_op jit(solution)/shard_map/all_gather | solution.py:198
  217.4 118.3 %all-gather.16.cloned.1.call-start = ((), (), s32[]{:S(2)}) async-start(), calls=%async_computation.15 | async-start | bytes 1622016 | tf_op jit(solution)/shard_map/all_gather | solution.py:114
  218.2 145.3 %all-gather.18.cloned.1.call-start = ((), (), s32[]{:S(2)}) async-start(), calls=%async_computation.16 | async-start | bytes 1622016 | tf_op jit(solution)/shard_map/all_gather | solution.py:115
  220.0 171.5 %all-gather.20.cloned.1.call-start = ((), (), s32[]{:S(2)}) async-start(), calls=%async_computation.17 | async-start | bytes 1622016 | tf_op jit(solution)/shard_map/all_gather | solution.py:116
  221.7 271.2 %reduce-scatter.17.cloned.1.call-start = ((), (), s32[]{:S(2)}) async-start(), calls=%async_computation.20 | async-start | bytes 5242880 | tf_op jit(solution)/shard_map/reduce_scatter | solution.py:231
  391.4 6.8 copy-start.56
  398.2 1.9 copy-start.29
  398.2 1.9 copy-start.27
  398.2 2.4 copy-start.57
  416.0 78.9 %copy-start.19 = (bf16[128,2,1024]{2,1,0:T(2,128)(2,1)S(1)}, bf16[128,2,1024]{2,1,0:T(2,128)(2,1)}, u32[]{:S(2)}) copy-start(bf16[128,2,1024]{2,1,0:T(2,128)(2,1)} %param.27) | copy-start | bytes 1572868
  416.0 127.0 %all-gather.24.cloned.1.call-start = ((), (), s32[]{:S(2)}) async-start(), calls=%async_computation.21 | async-start | bytes 2621440 | tf_op jit(solution)/shard_map/all_gather | solution.py:236
  492.9 2.0 copy-start.2
  492.9 2.2 copy-start.10
  496.4 150.7 %reduce-scatter.19.cloned.1.call-start = ((), (), s32[]{:S(2)}) async-start(), calls=%async_computation.22 | async-start | bytes 2621440 | tf_op jit(solution)/shard_map/reduce_scatter | solution.py:326
  506.5 36.4 %copy-start.24 = (bf16[256,1024]{1,0:T(8,128)(2,1)S(1)}, bf16[256,1024]{1,0:T(8,128)(2,1)}, u32[]{:S(2)}) copy-start(bf16[256,1024]{1,0:T(8,128)(2,1)} %all_gather.74) | copy-start | bytes 1572868
  543.0 4.0 copy-start.6
  551.4 1.8 copy-start.5
  554.6 7.8 copy-start.18
  565.9 4.1 copy-start.32
  565.9 4.1 copy-start.33
  573.3 3.8 copy-start.31
  578.2 2.8 copy-start.40
  578.2 2.8 copy-start.45
  578.2 3.9 copy-start.35
  590.0 3.7 copy-start.47
  593.7 87.9 %reduce-scatter.15.cloned.1.call-start = ((), (), s32[]{:S(2)}) async-start(), calls=%async_computation.18 | async-start | bytes 2621440 | tf_op jit(solution)/shard_map/reduce_scatter | solution.py:207
  602.9 126.7 %reduce-scatter.31.cloned.1.call-start = ((), (), s32[]{:S(2)}) async-start(), calls=%async_computation.28 | async-start | bytes 3244032 | tf_op jit(solution)/shard_map/reduce_scatter | solution.py:339
  609.1 169.8 %reduce-scatter.33.cloned.1.call-start = ((), (), s32[]{:S(2)}) async-start(), calls=%async_computation.29 | async-start | bytes 3244032 | tf_op jit(solution)/shard_map/reduce_scatter | solution.py:340
  615.3 1.6 copy-start.7
  615.4 212.3 %reduce-scatter.35.cloned.1.call-start = ((), (), s32[]{:S(2)}) async-start(), calls=%async_computation.30 | async-start | bytes 3244032 | tf_op jit(solution)/shard_map/reduce_scatter | solution.py:341
  621.6 2.4 copy-start.12
  621.7 245.9 %reduce-scatter.29.cloned.1.call-start = ((), (), s32[]{:S(2)}) async-start(), calls=%async_computation.27 | async-start | bytes 1179648 | tf_op jit(solution)/shard_map/reduce_scatter | solution.py:338
  630.3 2.9 copy-start.44
  633.1 3.5 copy-start.43
  633.1 274.5 %reduce-scatter.23.cloned.1.call-start = ((), (), s32[]{:S(2)}) async-start(), calls=%async_computation.24 | async-start | bytes 1179648 | tf_op jit(solution)/shard_map/reduce_scatter | solution.py:335
  636.6 3.5 copy-start.41
  636.6 311.0 %reduce-scatter.21.cloned.1.call-start = ((), (), s32[]{:S(2)}) async-start(), calls=%async_computation.23 | async-start | bytes 1179648 | tf_op jit(solution)/shard_map/reduce_scatter | solution.py:334
  640.1 3.5 copy-start.39
  640.1 347.5 %reduce-scatter.25.cloned.1.call-start = ((), (), s32[]{:S(2)}) async-start(), calls=%async_computation.25 | async-start | bytes 1179648 | tf_op jit(solution)/shard_map/reduce_scatter | solution.py:336
  643.5 384.1 %reduce-scatter.27.cloned.1.call-start = ((), (), s32[]{:S(2)}) async-start(), calls=%async_computation.26 | async-start | bytes 1179648 | tf_op jit(solution)/shard_map/reduce_scatter | solution.py:337
  643.6 38.0 %copy-start.20 = (bf16[128,2,1024]{2,1,0:T(2,128)(2,1)S(1)}, bf16[128,2,1024]{2,1,0:T(2,128)(2,1)}, u32[]{:S(2)}) copy-start(bf16[128,2,1024]{2,1,0:T(2,128)(2,1)} %param.27) | copy-start | bytes 1572868
  647.0 34.6 %copy-start.3 = (f32[128,2,1024]{2,0,1:T(8,128)S(1)}, f32[128,2,1024]{2,0,1:T(8,128)}, u32[]{:S(2)}) copy-start(f32[128,2,1024]{2,0,1:T(8,128)} %reduce-scatter.13.cloned.1.call-done) | copy-start | bytes 3145732
  647.0 34.6 %copy-start.11 = (f32[128,2,1024]{2,0,1:T(8,128)S(1)}, f32[128,2,1024]{2,0,1:T(8,128)}, u32[]{:S(2)}) copy-start(f32[128,2,1024]{2,0,1:T(8,128)} %reduce-scatter.17.cloned.1.call-done) | copy-start | bytes 3145732
  (13 other events, 15.6 us)
Sparse Core Ops, SparseCore 0:
  10.8 48.6 all-gather.11
  133.6 81.2 reduce-scatter.12
  216.5 46.4 all-gather.21
  264.5 44.6 all-gather.13
  311.7 24.0 all-gather.15
  338.2 25.2 all-gather.17
  366.1 25.2 all-gather.19
  416.1 76.7 reduce-scatter.16
  496.5 46.4 all-gather.23
  593.8 42.1 reduce-scatter.18
  638.4 43.1 reduce-scatter.14
  685.4 44.1 reduce-scatter.30
  734.0 44.8 reduce-scatter.32
  782.7 44.8 reduce-scatter.34
  831.5 36.0 reduce-scatter.28
  871.5 36.0 reduce-scatter.22
  911.5 36.0 reduce-scatter.20
  951.5 35.9 reduce-scatter.24
  991.6 35.9 reduce-scatter.26
where the time goes:
time: 1040 us; the launch traced here: 1030 us
  waiting for transfers between devices  710 us (68%)
  matrix products  107 us (10%)
  local copies, waits for them, and re-layouts  92.6 us (9%)
  blocking collectives  87 us (8%)
  other arithmetic  21.5 us (2%)
  between operations  15.3 us (1%)
    reduce_scatter x1, waiting for transfers between devices, shards(): lax.psum_scatter(jnp.dot(piece_rows, full_out, preferred_element_type=jnp...  80.6 us
    reduce_scatter x1, waiting for transfers between devices, shards(): lax.psum_scatter(summed.reshape(row_count, seq_count, model_width), 'tp',...  76.9 us
    reduce_scatter x1, waiting for transfers between devices, shards(): lax.psum_scatter(grad_right, ('fsdp', 'ctx'), scatter_dimension=0, tiled=...  49.2 us
    reduce_scatter x1, waiting for transfers between devices, shards(): lax.psum_scatter(grad_down, ('fsdp', 'ctx'), scatter_dimension=1, tiled=T...  48.7 us
    reduce_scatter x1, waiting for transfers between devices, shards(): lax.psum_scatter(grad_left, ('fsdp', 'ctx'), scatter_dimension=0, tiled=T...  43 us
    all_gather x1, waiting for transfers between devices, shards(): second = lax.all_gather(second_part, 'tp', axis=0, tiled=True)  42.1 us
    all_gather x1, waiting for transfers between devices, shards(): lax.all_gather(cotangent, 'tp', axis=0, tiled=True)  41.2 us
    reduce_scatter x1, waiting for transfers between devices, shards(): lax.psum_scatter(grad_wgate, ('fsdp', 'ctx'), scatter_dimension=0, tiled=...  40.1 us
  transfers between devices with their start and end apart: 19, of which 17 were waited for; matrix products, arithmetic and copies ran while one was open for 9% of the time, Pallas kernels for 0%

commit v1 on v0

--- a/solution.py
+++ b/solution.py
@@ -7,6 +7,24 @@
 EPSILON = 1e-06
 HEAD_FLOOR = 1.0
 HIGHEST = lax.Precision.HIGHEST
+
+
+def gather_around(shard, axis, dim):
+    ways, here, step = (lax.axis_size(axis), lax.axis_index(axis), shard.shape[dim])
+    shape = [n * ways if d == dim else n for d, n in enumerate(shard.shape)]
+    full = lax.dynamic_update_slice_in_dim(
+        jnp.zeros(shape, shard.dtype), shard, here * step, axis=dim
+    )
+    going_up = going_down = shard
+    for far in range(1, ways // 2 + 1):
+        going_up = lax.ppermute(going_up, axis, [(d, (d + 1) % ways) for d in range(ways)])
+        full = lax.dynamic_update_slice_in_dim(full, going_up, (here - far) % ways * step, axis=dim)
+        if 2 * far < ways:
+            going_down = lax.ppermute(going_down, axis, [(d, (d - 1) % ways) for d in range(ways)])
+            full = lax.dynamic_update_slice_in_dim(
+                full, going_down, (here + far) % ways * step, axis=dim
+            )
+    return full
 
 
 def entering(x, axis, join, neutral):
@@ -113,7 +131,7 @@
         lax.all_gather(w_out.astype(jnp.bfloat16), ("fsdp", "ctx"), axis=1, tiled=True),
         lax.all_gather(glu_left.astype(jnp.bfloat16), ("fsdp", "ctx"), axis=0, tiled=True),
         lax.all_gather(glu_right.astype(jnp.bfloat16), ("fsdp", "ctx"), axis=0, tiled=True),
-        lax.all_gather(glu_down.astype(jnp.bfloat16), ("fsdp", "ctx"), axis=1, tiled=True),
+        gather_around(glu_down.astype(jnp.bfloat16), ("fsdp", "ctx"), 1),
     )
     full_query, full_key, full_value, full_gate, full_out, full_left, full_right, full_down = (
         gathered

time: 1040 us -> 1020 us (0.981)
  waiting for transfers between devices: 710 us -> 672 us
    all_gather x1, waiting for transfers between devices: 41.2 us -> 15.9 us  [shards(): lax.all_gather(cotangent, 'tp', axis=0, tiled=True)]
    all_gather x1 -> x0, waiting for transfers between devices: 22.7 us -> none  [shards(): lax.all_gather(glu_down.astype(jnp.bfloat16), ('fsdp', 'ctx'), axis=1, ti...]
    ppermute x0 -> x7, waiting for transfers between devices: none -> 10.6 us  [the longest x4 10.4 us: gather_around(): lax.ppermute(going_up, axis, [(d, (d + 1) % ways) for d in range(ways)])]
  transfers between devices with their start and end apart: 19 -> 25, of which waited for: 17 -> 21; matrix products, arithmetic and copies ran while one was open for 9% -> 10% of each run, Pallas kernels for 0% -> 0%
where the time goes in v1:
time: 1020 us; the launch traced here: 1010 us
  waiting for transfers between devices  672 us (66%)
  matrix products  107 us (10%)
  local copies, waits for them, and re-layouts  97.3 us (10%)
  blocking collectives  87.4 us (9%)
  other arithmetic  23.5 us (2%)
  between operations  15.6 us (2%)
    reduce_scatter x1, waiting for transfers between devices, shards(): lax.psum_scatter(jnp.dot(piece_rows, full_out, preferred_element_type=jnp...  80.6 us
    reduce_scatter x1, waiting for transfers between devices, shards(): lax.psum_scatter(summed.reshape(row_count, seq_count, model_width), 'tp',...  76.9 us
    reduce_scatter x1, waiting for transfers between devices, shards(): lax.psum_scatter(grad_right, ('fsdp', 'ctx'), scatter_dimension=0, tiled=...  49.1 us
    reduce_scatter x1, waiting for transfers between devices, shards(): lax.psum_scatter(grad_down, ('fsdp', 'ctx'), scatter_dimension=1, tiled=T...  48.9 us
    reduce_scatter x1, waiting for transfers between devices, shards(): lax.psum_scatter(grad_left, ('fsdp', 'ctx'), scatter_dimension=0, tiled=T...  43.2 us
    all_gather x1, waiting for transfers between devices, shards(): second = lax.all_gather(second_part, 'tp', axis=0, tiled=True)  42.1 us
    reduce_scatter x1, waiting for transfers between devices, shards(): lax.psum_scatter(grad_wgate, ('fsdp', 'ctx'), scatter_dimension=0, tiled=...  40 us
    reduce_scatter x1, waiting for transfers between devices, shards(): lax.psum_scatter(grad_wquery, ('fsdp', 'ctx'), scatter_dimension=0, tiled...  40 us
  transfers between devices with their start and end apart: 25, of which 21 were waited for; matrix products, arithmetic and copies ran while one was open for 10% of the time, Pallas kernels for 0%

profile of v1, /device:TPU:0, one launch (start us, length us, event | category | flops | bytes accessed | tf_op | source)
XLA Modules:
  0.0 1013.4 jit_solution(14438286218828970677)
XLA Ops:
  11.0 6.0 all-gather.3
  17.2 5.3 all-gather.2
  22.5 5.0 all_gather.69
  28.1 10.1 all_gather.64
  38.2 9.8 all_gather.62
  48.0 9.9 all_gather.63
  57.9 10.7 %all_gather.70 = bf16[1024,256]{1,0:T(8,128)(2,1)} all-gather(bf16[128,256]{1,0:T(8,128)(2,1)S(1)} %convert_element_type.256), channel_id=1, replica_groups=mesh['fsdp'=2,'ctx'=4,'tp'=4] {'fsdp','ctx'}, dimensions={0}, use_global_device_ids=true | all-gather | bytes 589824 | tf_op jit(solution)/shard_map/all_gather | solution.py:130
  68.7 10.1 all_gather.71
  81.0 5.1 copy.98
  86.1 4.1 reshape.419
  90.2 3.7 add_multiply_fusion
  97.2 3.3 convolution_convert_fusion.1
  102.0 7.8 all-gather
  110.1 3.6 add_multiply_fusion.1
  133.4 80.6 %reduce-scatter.13.cloned.1.call-done = f32[128,2,1024]{2,0,1:T(8,128)} async-done(((f32[512,2,1024]{2,0,1:T(8,128)}), f32[128,2,1024]{2,0,1:T(8,128)}) %reduce-scatter.13.cloned.1.call-update) | async-done | bytes 1048592 | tf_op jit(solution)/shard_map/reduce_scatter | solution.py:206
  224.0 3.5 collective-permute-done
  227.5 3.0 collective-permute-start.3
  233.6 3.2 collective-permute-start.5
  241.1 4.4 collective-permute-done.6
  246.2 15.9 %all-gather.19.cloned.1.call-done = bf16[512,2,1024]{2,1,0:T(2,128)(2,1)} async-done(((bf16[128,2,1024]{2,1,0:T(2,128)(2,1)}), bf16[512,2,1024]{2,1,0:T(2,128)(2,1)}) %all-gather.19.cloned.1.call-update) | async-done | bytes 2097168 | tf_op jit(solution)/shard_map/all_gather | solution.py:234
  262.1 4.1 reshape.425
  266.2 42.1 %all-gather.13.cloned.1.call-done = bf16[512,2,1024]{2,0,1:T(8,128)(2,1)} async-done(((bf16[128,2,1024]{2,0,1:T(8,128)(2,1)}), bf16[512,2,1024]{2,0,1:T(8,128)(2,1)}) %all-gather.13.cloned.1.call-update) | async-done | bytes 2097168 | tf_op jit(solution)/shard_map/all_gather | solution.py:216
  308.3 5.1 copy.112
  313.4 4.2 reshape.424
  317.6 17.3 %all-gather.15.cloned.1.call-done = bf16[1024,704]{0,1:T(8,128)(2,1)} async-done(((bf16[128,704]{0,1:T(8,128)(2,1)}), bf16[1024,704]{0,1:T(8,128)(2,1)}) %all-gather.15.cloned.1.call-update) | async-done | bytes 1441808 | tf_op jit(solution)/shard_map/all_gather | solution.py:132
  334.8 5.2 fusion.70
  340.0 22.6 %all-gather.17.cloned.1.call-done = bf16[1024,704]{0,1:T(8,128)(2,1)} async-done(((bf16[128,704]{0,1:T(8,128)(2,1)}), bf16[1024,704]{0,1:T(8,128)(2,1)}) %all-gather.17.cloned.1.call-update) | async-done | bytes 1441808 | tf_op jit(solution)/shard_map/all_gather | solution.py:133
  362.6 3.8 fusion.71
  366.5 4.6 fusion.4
  373.5 4.0 convolution_add_fusion
  377.4 6.0 reshape.426
  383.4 5.5 copy.115
  389.0 76.9 %reduce-scatter.17.cloned.1.call-done = f32[128,2,1024]{2,0,1:T(8,128)} async-done(((f32[512,2,1024]{2,0,1:T(8,128)}), f32[128,2,1024]{2,0,1:T(8,128)}) %reduce-scatter.17.cloned.1.call-update) | async-done | bytes 1048592 | tf_op jit(solution)/shard_map/reduce_scatter | solution.py:249
  469.5 5.0 all_gather.79
  474.6 2.8 reshape.428
  479.6 2.8 reshape.427
  484.7 31.3 %all-gather.21.cloned.1.call-done = bf16[512,2,1024]{2,0,1:T(8,128)(2,1)} async-done(((bf16[128,2,1024]{2,0,1:T(8,128)(2,1)}), bf16[512,2,1024]{2,0,1:T(8,128)(2,1)}) %all-gather.21.cloned.1.call-update) | async-done | bytes 2097168 | tf_op jit(solution)/shard_map/all_gather | solution.py:254
  516.0 4.0 multiply_reduce_fusion
  527.7 7.7 all-gather.1
  535.5 3.2 while.30
  542.9 4.0 fusion.43
  549.4 4.0 fusion.47
  556.2 4.1 fusion.39
  561.4 5.6 add_convert_fusion
  569.2 3.5 copy.135
  574.1 4.5 convolution_convert_fusion
  585.0 4.6 fusion.75
  589.6 4.6 fusion.76
  595.8 4.6 fusion.74
  602.9 3.4 copy.137
  609.1 2.9 fusion.31
  612.0 3.4 fusion.41
  615.5 3.4 fusion.45
  619.0 3.3 fusion.37
  622.5 3.4 fusion.34
  627.3 32.7 %reduce-scatter.15.cloned.1.call-done = bf16[128,2,1024]{2,0,1:T(8,128)(2,1)} async-done(((bf16[512,2,1024]{2,0,1:T(8,128)(2,1)}), bf16[128,2,1024]{2,0,1:T(8,128)(2,1)}) %reduce-scatter.15.cloned.1.call-update) | async-done | bytes 524304 | tf_op jit(solution)/shard_map/reduce_scatter | solution.py:225
  665.1 43.2 %reduce-scatter.31.cloned.1.call-done = f32[128,704]{0,1:T(8,128)} async-done(((f32[1024,704]{0,1:T(8,128)}), f32[128,704]{0,1:T(8,128)}) %reduce-scatter.31.cloned.1.call-update) | async-done | bytes 360464 | tf_op jit(solution)/shard_map/reduce_scatter | solution.py:357
  708.2 49.1 %reduce-scatter.33.cloned.1.call-done = f32[128,704]{0,1:T(8,128)} async-done(((f32[1024,704]{0,1:T(8,128)}), f32[128,704]{0,1:T(8,128)}) %reduce-scatter.33.cloned.1.call-update) | async-done | bytes 360464 | tf_op jit(solution)/shard_map/reduce_scatter | solution.py:358
  757.3 48.9 %reduce-scatter.35.cloned.1.call-done = f32[704,128]{1,0:T(8,128)} async-done(((f32[704,1024]{1,0:T(8,128)}), f32[704,128]{1,0:T(8,128)}) %reduce-scatter.35.cloned.1.call-update) | async-done | bytes 360464 | tf_op jit(solution)/shard_map/reduce_scatter | solution.py:359
  806.2 40.0 %reduce-scatter.29.cloned.1.call-done = f32[256,128]{1,0:T(8,128)} async-done(((f32[256,1024]{1,0:T(8,128)}), f32[256,128]{1,0:T(8,128)}) %reduce-scatter.29.cloned.1.call-update) | async-done | bytes 131088 | tf_op jit(solution)/shard_map/reduce_scatter | solution.py:356
  846.2 40.0 %reduce-scatter.23.cloned.1.call-done = f32[128,256]{1,0:T(8,128)} async-done(((f32[1024,256]{1,0:T(8,128)}), f32[128,256]{1,0:T(8,128)}) %reduce-scatter.23.cloned.1.call-update) | async-done | bytes 131088 | tf_op jit(solution)/shard_map/reduce_scatter | solution.py:353
  886.2 40.0 %reduce-scatter.21.cloned.1.call-done = f32[128,256]{1,0:T(8,128)} async-done(((f32[1024,256]{1,0:T(8,128)}), f32[128,256]{1,0:T(8,128)}) %reduce-scatter.21.cloned.1.call-update) | async-done | bytes 131088 | tf_op jit(solution)/shard_map/reduce_scatter | solution.py:352
  926.2 40.0 %reduce-scatter.25.cloned.1.call-done = f32[128,256]{1,0:T(8,128)} async-done(((f32[1024,256]{1,0:T(8,128)}), f32[128,256]{1,0:T(8,128)}) %reduce-scatter.25.cloned.1.call-update) | async-done | bytes 131088 | tf_op jit(solution)/shard_map/reduce_scatter | solution.py:354
  966.1 40.0 %reduce-scatter.27.cloned.1.call-done = f32[128,256]{1,0:T(8,128)} async-done(((f32[1024,256]{1,0:T(8,128)}), f32[128,256]{1,0:T(8,128)}) %reduce-scatter.27.cloned.1.call-update) | async-done | bytes 131088 | tf_op jit(solution)/shard_map/reduce_scatter | solution.py:355
  (270 shorter events, 104.6 us)
Async XLA Ops:
  7.2 3.6 copy-start.57
  7.2 10.0 copy-start.58
  7.2 20.4 %copy-start.52 = (f32[128,256]{1,0:T(8,128)S(1)}, f32[128,256]{1,0:T(8,128)}, u32[]{:S(2)}) copy-start(f32[128,256]{1,0:T(8,128)} %param.20) | copy-start | bytes 393220
  7.2 20.4 %copy-start.53 = (f32[128,256]{1,0:T(8,128)S(1)}, f32[128,256]{1,0:T(8,128)}, u32[]{:S(2)}) copy-start(f32[128,256]{1,0:T(8,128)} %param.21) | copy-start | bytes 393220
  7.2 20.6 %copy-start.54 = (f32[128,256]{1,0:T(8,128)S(1)}, f32[128,256]{1,0:T(8,128)}, u32[]{:S(2)}) copy-start(f32[128,256]{1,0:T(8,128)} %param.19) | copy-start | bytes 393220
  7.2 20.6 %copy-start.55 = (f32[128,256]{1,0:T(8,128)S(1)}, f32[128,256]{1,0:T(8,128)}, u32[]{:S(2)}) copy-start(f32[128,256]{1,0:T(8,128)} %param.22) | copy-start | bytes 393220
  7.2 20.6 %copy-start.56 = (f32[256,128]{1,0:T(8,128)S(1)}, f32[256,128]{1,0:T(8,128)}, u32[]{:S(2)}) copy-start(f32[256,128]{1,0:T(8,128)} %param.23) | copy-start | bytes 393220
  7.2 73.7 %all-gather.11.cloned.1.call-start = ((), (), s32[]{:S(2)}) async-start(), calls=%async_computation.12 | async-start | bytes 2621440 | tf_op jit(solution)/shard_map/all_gather | solution.py:139
  10.7 203.3 %reduce-scatter.13.cloned.1.call-start = ((), (), s32[]{:S(2)}) async-start(), calls=%async_computation.13 | async-start | bytes 5242880 | tf_op jit(solution)/shard_map/reduce_scatter | solution.py:206
  38.2 52.0 %copy-start.36 = (bf16[1024,256]{1,0:T(8,128)(2,1)}, bf16[1024,256]{1,0:T(8,128)(2,1)S(1)}, u32[]{:S(2)}) copy-start(bf16[1024,256]{1,0:T(8,128)(2,1)S(1)} %all_gather.64) | copy-start | bytes 1572868
  48.0 49.2 %copy-start.35 = (bf16[1024,256]{1,0:T(8,128)(2,1)}, bf16[1024,256]{1,0:T(8,128)(2,1)S(1)}, u32[]{:S(2)}) copy-start(bf16[1024,256]{1,0:T(8,128)(2,1)S(1)} %all_gather.62) | copy-start | bytes 1572868
  97.2 18.7 %copy-start.14 = (bf16[512,2,2,128]{0,3,2,1:T(8,128)(2,1)}, bf16[512,2,2,128]{0,3,2,1:T(8,128)(2,1)S(1)}, u32[]{:S(2)}) copy-start(bf16[512,2,2,128]{0,3,2,1:T(8,128)(2,1)S(1)} %copy.103) | copy-start | bytes 1572868
  101.7 8.1 copy-start.17
  115.9 3.2 copy-start.7
  125.7 4.1 copy-start.25
  132.6 81.4 %copy-start = (bf16[128,2,1024]{2,1,0:T(2,128)(2,1)S(1)}, bf16[128,2,1024]{2,1,0:T(2,128)(2,1)}, u32[]{:S(2)}) copy-start(bf16[128,2,1024]{2,1,0:T(2,128)(2,1)} %param.16) | copy-start | bytes 1572868
  132.6 129.5 %all-gather.19.cloned.1.call-start = ((), (), s32[]{:S(2)}) async-start(), calls=%async_computation.18 | async-start | bytes 2621440 | tf_op jit(solution)/shard_map/all_gather | solution.py:234
  133.3 83.4 %copy-start.50 = (f32[128,704]{0,1:T(8,128)S(1)}, f32[128,704]{0,1:T(8,128)}, u32[]{:S(2)}) copy-start(f32[128,704]{0,1:T(8,128)} %param.24) | copy-start | bytes 1081348
  133.3 175.0 %all-gather.13.cloned.1.call-start = ((), (), s32[]{:S(2)}) async-start(), calls=%async_computation.14 | async-start | bytes 2621440 | tf_op jit(solution)/shard_map/all_gather | solution.py:216
  216.6 118.2 %all-gather.15.cloned.1.call-start = ((), (), s32[]{:S(2)}) async-start(), calls=%async_computation.15 | async-start | bytes 1622016 | tf_op jit(solution)/shard_map/all_gather | solution.py:132
  217.4 3.2 copy-start.51
  217.4 145.2 %all-gather.17.cloned.1.call-start = ((), (), s32[]{:S(2)}) async-start(), calls=%async_computation.16 | async-start | bytes 1622016 | tf_op jit(solution)/shard_map/all_gather | solution.py:133
  219.2 246.7 %reduce-scatter.17.cloned.1.call-start = ((), (), s32[]{:S(2)}) async-start(), calls=%async_computation.19 | async-start | bytes 5242880 | tf_op jit(solution)/shard_map/reduce_scatter | solution.py:249
  221.4 6.1 collective-permute-start
  221.4 6.1 collective-permute-start.1
  227.5 5.9 collective-permute-start.2
  227.5 6.0 collective-permute-start.3
  233.4 5.9 collective-permute-start.4
  233.6 6.8 collective-permute-start.5
  239.3 6.2 collective-permute-start.6
  362.6 3.8 copy-start.12
  362.6 3.8 copy-start.32
  366.5 4.6 copy-start.59
  389.0 78.9 %copy-start.21 = (bf16[128,2,1024]{2,1,0:T(2,128)(2,1)S(1)}, bf16[128,2,1024]{2,1,0:T(2,128)(2,1)}, u32[]{:S(2)}) copy-start(bf16[128,2,1024]{2,1,0:T(2,128)(2,1)} %param.27) | copy-start | bytes 1572868
  389.0 127.0 %all-gather.21.cloned.1.call-start = ((), (), s32[]{:S(2)}) async-start(), calls=%async_computation.20 | async-start | bytes 2621440 | tf_op jit(solution)/shard_map/all_gather | solution.py:254
  469.4 156.5 %reduce-scatter.19.cloned.1.call-start = ((), (), s32[]{:S(2)}) async-start(), calls=%async_computation.21 | async-start | bytes 2621440 | tf_op jit(solution)/shard_map/reduce_scatter | solution.py:344
  479.6 36.4 %copy-start.26 = (bf16[256,1024]{1,0:T(8,128)(2,1)S(1)}, bf16[256,1024]{1,0:T(8,128)(2,1)}, u32[]{:S(2)}) copy-start(bf16[256,1024]{1,0:T(8,128)(2,1)} %all_gather.71) | copy-start | bytes 1572868
  516.0 4.1 copy-start.6
  527.7 10.9 %copy-start.20 = (bf16[512,2,2,128]{3,2,1,0:T(2,128)(2,1)S(1)}, bf16[512,2,2,128]{3,2,1,0:T(2,128)(2,1)}, u32[]{:S(2)}) copy-start(bf16[512,2,2,128]{3,2,1,0:T(2,128)(2,1)} %copy-done.17) | copy-start | bytes 1572868
  527.7 11.0 %copy-start.30 = (f32[512,2,2,128]{0,3,2,1:T(8,128)S(1)}, f32[512,2,2,128]{0,3,2,1:T(8,128)}, u32[]{:S(2)}) copy-start(f32[512,2,2,128]{0,3,2,1:T(8,128)} %convolution_bitcast_fusion) | copy-start | bytes 3145732
  542.9 4.0 copy-start.42
  542.9 4.0 copy-start.29
  542.9 4.0 copy-start.31
  549.4 4.1 copy-start.40
  549.4 4.0 copy-start.16
  549.4 4.0 copy-start.28
  556.2 4.1 copy-start.38
  556.2 4.1 copy-start.44
  556.2 5.2 copy-start.34
  572.8 87.3 %reduce-scatter.15.cloned.1.call-start = ((), (), s32[]{:S(2)}) async-start(), calls=%async_computation.17 | async-start | bytes 2621440 | tf_op jit(solution)/shard_map/reduce_scatter | solution.py:225
  583.4 124.9 %reduce-scatter.31.cloned.1.call-start = ((), (), s32[]{:S(2)}) async-start(), calls=%async_computation.27 | async-start | bytes 3244032 | tf_op jit(solution)/shard_map/reduce_scatter | solution.py:357
  589.5 167.8 %reduce-scatter.33.cloned.1.call-start = ((), (), s32[]{:S(2)}) async-start(), calls=%async_computation.28 | async-start | bytes 3244032 | tf_op jit(solution)/shard_map/reduce_scatter | solution.py:358
  594.2 212.0 %reduce-scatter.35.cloned.1.call-start = ((), (), s32[]{:S(2)}) async-start(), calls=%async_computation.29 | async-start | bytes 3244032 | tf_op jit(solution)/shard_map/reduce_scatter | solution.py:359
  600.5 245.7 %reduce-scatter.29.cloned.1.call-start = ((), (), s32[]{:S(2)}) async-start(), calls=%async_computation.26 | async-start | bytes 1179648 | tf_op jit(solution)/shard_map/reduce_scatter | solution.py:356
  612.0 3.5 copy-start.41
  612.0 274.2 %reduce-scatter.23.cloned.1.call-start = ((), (), s32[]{:S(2)}) async-start(), calls=%async_computation.23 | async-start | bytes 1179648 | tf_op jit(solution)/shard_map/reduce_scatter | solution.py:353
  615.4 3.6 copy-start.39
  615.4 310.7 %reduce-scatter.21.cloned.1.call-start = ((), (), s32[]{:S(2)}) async-start(), calls=%async_computation.22 | async-start | bytes 1179648 | tf_op jit(solution)/shard_map/reduce_scatter | solution.py:352
  619.0 3.5 copy-start.37
  619.0 347.2 %reduce-scatter.25.cloned.1.call-start = ((), (), s32[]{:S(2)}) async-start(), calls=%async_computation.24 | async-start | bytes 1179648 | tf_op jit(solution)/shard_map/reduce_scatter | solution.py:354
  622.4 383.8 %reduce-scatter.27.cloned.1.call-start = ((), (), s32[]{:S(2)}) async-start(), calls=%async_computation.25 | async-start | bytes 1179648 | tf_op jit(solution)/shard_map/reduce_scatter | solution.py:355
  622.4 37.6 %copy-start.22 = (bf16[128,2,1024]{2,1,0:T(2,128)(2,1)S(1)}, bf16[128,2,1024]{2,1,0:T(2,128)(2,1)}, u32[]{:S(2)}) copy-start(bf16[128,2,1024]{2,1,0:T(2,128)(2,1)} %param.27) | copy-start | bytes 1572868
  625.8 34.2 %copy-start.3 = (f32[128,2,1024]{2,0,1:T(8,128)S(1)}, f32[128,2,1024]{2,0,1:T(8,128)}, u32[]{:S(2)}) copy-start(f32[128,2,1024]{2,0,1:T(8,128)} %reduce-scatter.13.cloned.1.call-done) | copy-start | bytes 3145732
  625.8 34.2 %copy-start.10 = (f32[128,2,1024]{2,0,1:T(8,128)S(1)}, f32[128,2,1024]{2,0,1:T(8,128)}, u32[]{:S(2)}) copy-start(f32[128,2,1024]{2,0,1:T(8,128)} %reduce-scatter.17.cloned.1.call-done) | copy-start | bytes 3145732
  (22 other events, 40.2 us)
Sparse Core Ops, SparseCore 0:
  10.8 48.6 all-gather.10
  132.7 81.2 reduce-scatter.12
  215.7 46.4 all-gather.18
  263.6 44.6 all-gather.12
  310.8 24.0 all-gather.14
  337.3 25.2 all-gather.16
  389.1 76.7 reduce-scatter.16
  469.5 46.4 all-gather.20
  572.9 41.6 reduce-scatter.18
  616.8 43.1 reduce-scatter.14
  664.0 44.2 reduce-scatter.30
  712.4 44.8 reduce-scatter.32
  761.3 44.9 reduce-scatter.34
  810.2 35.9 reduce-scatter.28
  850.1 36.0 reduce-scatter.22
  890.1 36.0 reduce-scatter.20
  930.1 35.9 reduce-scatter.24
  970.1 36.0 reduce-scatter.26
